TPU v7x, 32 devices: a whole 2x2x4 slice. The times are simulated.
32 devices in a mesh: shock: 16 (over z, x, core), trans: 2 (over y).
Axes of the slice: x: 2, y: 2, z: 4, core: 2. Of those that a mesh axis runs over, the one named last changes fastest.
Arguments:
- displacement: float32 [3, 8192], P(None, ('shock', 'trans')), may hold values from -0.32 to 0.32
- velocity: float32 [3, 8192], P(None, ('shock', 'trans')), may hold values from -4 to 4
- force_before: float32 [3, 8192], P(None, ('shock', 'trans')), may hold values from -4 to 4
- beta: float32 [50], replicated, may hold values from -0.875 to 0.875
- alpha: float32 [50, 50], replicated, may hold values from -0.125 to 0.125
- live_count: int32 [32], P(('shock', 'trans')), may hold values from 128 to 256, as said below
- trans_send: int32 [2, 1024], P(None, ('shock', 'trans')), may hold values from 0 to 127, as said below
- shock_send: int32 [2, 4096], P(None, ('shock', 'trans')), may hold values from 0 to 319, as said below
- neighbour_block: int32 [26, 8192], P(None, ('shock', 'trans')), may hold values from -1 to 4, as said below
- neighbour_lane: int32 [26, 8192], P(None, ('shock', 'trans')), may hold values from 0 to 127, as said below
- leaving_slots: int32 [512], P(('shock', 'trans')), may hold values from 0 to 127, as said below
- leaving_count: int32 [32], P(('shock', 'trans')), may hold values from 8 to 16, as said below
Outputs:
- displacement_next: float32 [3, 8192], P(None, ('shock', 'trans'))
- velocity_next: float32 [3, 8192], P(None, ('shock', 'trans'))
- force_next: float32 [3, 8192], P(None, ('shock', 'trans'))
- atom_energy: float32 [8192], P(('shock', 'trans'))
- arrivals: float32 [3, 3, 512], P(None, None, ('shock', 'trans'))
Inputs may be any that keep to these rules, and one draw needn't show every extreme that they name: A store's live atoms are its slots 0 to live_count - 1; stores at the lowest shock indices, behind the front, are full, and some store holds 256. `trans_send`: entries are live atoms of the sending store. `shock_send`: entries are live atoms or transverse ghost columns of the sending store's first section. `neighbour_block`: -1 marks an absent neighbour; slots at or above live_count have none; otherwise the column names a live own atom or a ghost column, never a ghost block beyond an open end of the shock axis. `neighbour_lane`: read together with neighbour_block. `leaving_slots`: distinct live atoms of the store. `leaving_count`: some store uses all 16 entries.
All inputs are finite; a program needn't handle non-finite values.
Results may differ from a plain program's by a relative error of at most 0.0003.
Values sent between devices are 32-bit elements; how exact they have to be, the bound alone decides.
No kernel may reach another device: no remote copies, remote signals or barrier semaphores. Data moves between devices by JAX's collectives and lax.ppermute only.
A program may use at most 64 MiB of HBM per device.

v0:
```python
import math

import jax
import jax.numpy as jnp
from jax import lax
from jax.experimental import pallas as pl
from jax.experimental.pallas import tpu as pltpu
from jax.sharding import PartitionSpec as P


kick_factor = 0.5
drift_step = 0.02
cutoff_radius = 4.2
radial_width = 0.35
radial_centers = (1.4, 1.9, 2.4, 2.9)
moment_scale = 0.25
pair_list = ((0, 0), (0, 1), (0, 2), (0, 3), (1, 1), (1, 2), (1, 3), (2, 2), (2, 3), (3, 3))
degrees = 5
lanes = 128
highest = lax.Precision.HIGHEST
f32 = jnp.float32
bf16 = jnp.bfloat16


def lattice_list():
    entries = []
    for number in range(8):
        entries.append(
            (1.0 - 2.0 * (number >> 2 & 1), 1.0 - 2.0 * (number >> 1 & 1), 1.0 - 2.0 * (number & 1))
        )
    for axis_pick in range(3):
        for signed in (2.0, -2.0):
            vector = [0.0, 0.0, 0.0]
            vector[axis_pick] = signed
            entries.append(tuple(vector))
    for zero_pick in (2, 1, 0):
        others = [axis_pick for axis_pick in range(3) if axis_pick != zero_pick]
        for leading in (2.0, -2.0):
            for trailing in (2.0, -2.0):
                vector = [0.0, 0.0, 0.0]
                vector[others[0]] = leading
                vector[others[1]] = trailing
                entries.append(tuple(vector))
    return entries


def exponent_list():
    return [
        (p, q, degree - p - q)
        for degree in range(degrees)
        for p in range(degree, -1, -1)
        for q in range(degree - p, -1, -1)
    ]


exponents = exponent_list()


def rows_of(value, count=8):
    return jnp.broadcast_to(value, (count,) + value.shape[1:])


def pick_lanes(table, index):
    return jnp.take_along_axis(table, index, axis=1, mode="promise_in_bounds")


def pick_columns(blocks, column):
    rows = blocks[0].shape[0]
    lane = rows_of(column & (lanes - 1), rows)
    block = rows_of(column >> 7, rows)
    out = jnp.zeros((rows, lanes), f32)
    for number, table in enumerate(blocks):
        out = jnp.where(block == number, pick_lanes(table, lane), out)
    return out


def pad_lanes(value, fill=0):
    rows, width = value.shape
    if width == lanes:
        return value
    return jnp.concatenate([value, jnp.full((rows, lanes - width), fill, value.dtype)], axis=1)


def pad_rows(value, count=8):
    rows = value.shape[0]
    return jnp.concatenate([value, jnp.zeros((count - rows,) + value.shape[1:], value.dtype)], axis=0)


def scatter_product(items, block_count, marks=None):
    sub = lax.broadcasted_iota(jnp.int32, (8, lanes), 0)
    spot = lax.broadcasted_iota(jnp.int32, (lanes, lanes), 0)
    left = []
    right = []
    for value, lane, block in items:
        high = value.astype(bf16).astype(f32)
        part = jnp.where(sub < 3, high, value - high)
        block = rows_of(block)
        left.append(
            jnp.concatenate(
                [jnp.where(block == number, part, 0.0) for number in range(block_count)], axis=0
            ).astype(bf16)
        )
        if marks is not None:
            continue
        right.append(
            jnp.where(spot == jnp.broadcast_to(lane, (lanes, lanes)), 1.0, 0.0).astype(bf16)
        )
    return lax.dot_general(
        jnp.concatenate(left, axis=1),
        jnp.concatenate(right, axis=1) if marks is None else marks,
        (((1,), (1,)), ((), ())),
        preferred_element_type=f32,
    )


def twice(value):
    return jnp.concatenate([value, value, value[:2]], axis=0)


def summed(product, number):
    return product[8 * number : 8 * number + 3] + product[8 * number + 3 : 8 * number + 6]


def start_kernel(disp, vel, force, trans_send, displaced_out, trans_out):
    displaced = disp[...] + drift_step * (vel[...] + kick_factor * force[...])
    displaced_out[...] = displaced
    width = trans_send.shape[1]
    blocks = [
        pad_rows(displaced[:, lanes * b : lanes * (b + 1)]) for b in range(displaced.shape[1] // lanes)
    ]
    for way in range(2):
        column = pad_lanes(trans_send[way : way + 1, :])
        trans_out[way] = pick_columns(blocks, column)[:3, :width]


def prepare_kernel(
    shock_send,
    neighbour_block,
    neighbour_lane,
    beta,
    alpha,
    trans_like,
    shock_spots_out,
    spots_out,
    linear_out,
    matrix_out,
):
    neighbours, slots = neighbour_block.shape
    halves = slots // lanes
    width = trans_like.shape[2]
    column = neighbour_block[...] * lanes + neighbour_lane[...]
    column = jnp.where(column >= slots + 2 * width, column + (lanes - 2 * width), column)
    even = lax.axis_index("shock") % 2 == 0
    border = (halves + 1) * lanes
    turned = column + lanes * (2 * halves + 3) - 2 * (column & -lanes)
    column = jnp.where(even & (column >= border), turned, column)
    column = jnp.where(neighbour_block[...] < 0, -1, column)
    spots_out[...] = jnp.full(spots_out.shape, -1, jnp.int32)
    for number in range(halves):
        spots_out[pl.ds(number, neighbours, stride=halves), :] = column[
            :, lanes * number : lanes * (number + 1)
        ]
    shock_spots_out[0:1, :] = jnp.where(even, shock_send[1:2, :], shock_send[0:1, :])
    shock_spots_out[1:2, :] = jnp.where(even, shock_send[0:1, :], shock_send[1:2, :])
    matrix = alpha[...]
    count = matrix.shape[0]
    matrix_out[...] = 0.5 * (matrix + matrix.T)
    eye = lax.broadcasted_iota(jnp.int32, (count, count), 0) == lax.broadcasted_iota(
        jnp.int32, (count, count), 1
    )
    linear = jnp.sum(
        jnp.where(eye, jnp.broadcast_to(beta[...], (count, count)), 0.0), axis=1, keepdims=True
    )
    linear_out[...] = jnp.broadcast_to(linear, linear_out.shape)


def settle_kernel(
    counts,
    vel,
    force,
    trans_send,
    leaving_slots,
    after,
    half_out,
    kept_out,
    trans_spots_out,
    leaving_out,
):
    slots = vel.shape[1]
    half_out[...] = vel[...] + kick_factor * force[...]
    trans_spots_out[...] = pad_lanes(trans_send[...], -1)
    leaving = leaving_slots.shape[1]
    entry = lax.broadcasted_iota(jnp.int32, (1, leaving), 1)
    going = jnp.where(entry < jnp.broadcast_to(counts[:, 1:2], (1, leaving)), leaving_slots[...], -1)
    leaving_out[...] = pad_lanes(going, -1)
    square = (leaving, leaving)
    eye = lax.broadcasted_iota(jnp.int32, square, 0) == lax.broadcasted_iota(jnp.int32, square, 1)
    upright = jnp.sum(
        jnp.where(eye, jnp.broadcast_to(going, square).astype(f32), 0.0), axis=1, keepdims=True
    )
    slot = lax.broadcasted_iota(jnp.int32, (leaving, slots), 1)
    gone = jnp.where(slot.astype(f32) == jnp.broadcast_to(upright, slot.shape), 1.0, 0.0)
    gone = jnp.sum(gone, axis=0, keepdims=True)
    live = slot[:1] < jnp.broadcast_to(counts[:, 0:1], (1, slots))
    kept_out[...] = jnp.where(live, 1.0 - gone, 0.0)


def mark_kernel(spots, marks_out):
    spot = lax.broadcasted_iota(jnp.int32, (lanes, lanes), 0)
    for row in range(marks_out.shape[1] // lanes):
        lane = jnp.broadcast_to(spots[row : row + 1, :] & (lanes - 1), (lanes, lanes))
        marks_out[:, lanes * row : lanes * (row + 1)] = jnp.where(spot == lane, 1.0, 0.0).astype(bf16)


def shock_kernel(displaced, trans_in, shock_spots, first_out, second_out, trans_block):
    width = trans_in.shape[2]
    trans_block[...] = jnp.zeros(trans_block.shape, f32)
    trans_block[:3, :width] = trans_in[1]
    trans_block[:3, width : 2 * width] = trans_in[0]
    blocks = [
        pad_rows(displaced[:, lanes * b : lanes * (b + 1)]) for b in range(displaced.shape[1] // lanes)
    ]
    blocks.append(trans_block[...])
    for way, out in enumerate((first_out, second_out)):
        out[...] = pick_columns(blocks, shock_spots[way : way + 1, :])[:3]


def energy_kernel(
    displaced,
    trans_in,
    from_first,
    from_second,
    spots,
    linear,
    matrix,
    marks,
    energy_out,
    own_out,
    trans_out,
    first_out,
    second_out,
    trans_block,
    grads,
    packed,
):
    slots = displaced.shape[1]
    width = trans_in.shape[2]
    halves = slots // lanes
    per_group = 8 // halves
    groups = spots.shape[0] // 8
    own_blocks = halves
    block_count = own_blocks + 3
    sub = lax.broadcasted_iota(jnp.int32, (8, lanes), 0)
    half_of = sub % halves
    which = sub // halves

    def by_half(pieces):
        out = rows_of(pieces[0])
        for number in range(1, halves):
            out = jnp.where(half_of == number, rows_of(pieces[number]), out)
        return out

    def by_which(values):
        out = jnp.full((8, lanes), values[0], f32)
        for number in range(1, per_group):
            if any(v != values[0] for v in values):
                out = jnp.where(which == number, values[number], out)
        return out

    def over_group(value):
        shift = 4
        while shift >= halves:
            value = value + pltpu.roll(value, shift, 0)
            shift //= 2
        return value

    trans_block[...] = jnp.zeros(trans_block.shape, f32)
    trans_block[:3, :width] = trans_in[1]
    trans_block[:3, width : 2 * width] = trans_in[0]

    def table(axis):
        pieces = [displaced[axis : axis + 1, lanes * b : lanes * (b + 1)] for b in range(own_blocks)]
        pieces.append(trans_block[axis : axis + 1, :])
        pieces.append(from_first[axis : axis + 1, :])
        pieces.append(from_second[axis : axis + 1, :])
        return pieces

    tables = [table(axis) for axis in range(3)]
    own = [by_half(tables[axis][:own_blocks]) for axis in range(3)]
    spread = [[rows_of(piece) for piece in tables[axis]] for axis in range(3)]
    offsets = lattice_list()
    neighbours = len(offsets)
    offsets = offsets + [offsets[0]] * (groups * per_group - neighbours)

    directions = []
    radials = []
    slopes = []
    inverses = []
    for group in range(groups):
        spot = spots[8 * group : 8 * group + 8, :]
        live = spot >= 0
        lane = jnp.where(live, spot & (lanes - 1), 0)
        block = jnp.where(live, spot >> 7, 0)
        vector = []
        for axis in range(3):
            picked = pick_lanes(spread[axis][0], lane)
            for number in range(1, block_count):
                picked = jnp.where(block == number, pick_lanes(spread[axis][number], lane), picked)
            offset = by_which([offsets[per_group * group + i][axis] for i in range(per_group)])
            vector.append(offset + picked - own[axis])
        square = vector[0] * vector[0] + vector[1] * vector[1] + vector[2] * vector[2]
        inverse = lax.rsqrt(square)
        distance = square * inverse
        directions.append([v * inverse for v in vector])
        inverses.append(inverse)
        angle = distance * (math.pi / cutoff_radius) - (math.pi / 2)
        squared = angle * angle
        sine = jnp.full_like(angle, -1.0 / math.factorial(15))
        for order in (13, 11, 9, 7, 5, 3, 1):
            sine = sine * squared + ((-1.0) ** ((order - 1) // 2)) / math.factorial(order)
        sine = sine * angle
        cosine = jnp.full_like(angle, 1.0 / math.factorial(16))
        for order in (14, 12, 10, 8, 6, 4, 2, 0):
            cosine = cosine * squared + ((-1.0) ** (order // 2)) / math.factorial(order)
        half = jnp.where(live, 0.5, 0.0)
        smooth = half - half * sine
        smooth_slope = half * cosine * (-math.pi / cutoff_radius)
        radial = []
        slope = []
        for center in radial_centers:
            away = (distance - center) * (1.0 / radial_width)
            bell = jnp.exp(-away * away)
            radial.append(smooth * bell)
            slope.append(bell * (smooth_slope - smooth * away * (2.0 / radial_width)))
        radials.append(radial)
        slopes.append(slope)

    scaled = [
        [
            [direction[axis] * (1.0 / power) if power > 1 else direction[axis] for power in range(1, degrees)]
            for axis in range(3)
        ]
        for direction in directions
    ]
    monomials = {}
    kinds = len(radial_centers)
    moments = {}
    for triple in exponents:
        p, q, w = triple
        if p + q + w == 0:
            monomials[triple] = None
        else:
            axis = 0 if p else (1 if q else 2)
            lower = tuple(v - (1 if a == axis else 0) for a, v in enumerate(triple))
            values = []
            for group in range(groups):
                factor = scaled[group][axis][triple[axis] - 1]
                before = monomials[lower]
                values.append(factor if before is None else before[group] * factor)
            monomials[triple] = values
        for kind in range(kinds):
            total = None
            for group in range(groups):
                term = radials[group][kind]
                if monomials[triple] is not None:
                    term = term * monomials[triple][group]
                total = term if total is None else total + term
            moments[kind, triple] = over_group(total)

    weighted = {}
    for triple in exponents:
        weight = moment_scale**2 * math.factorial(sum(triple))
        for power in triple:
            weight *= math.factorial(power)
        for kind in range(kinds):
            weighted[kind, triple] = moments[kind, triple] * weight
    descriptor = []
    for first, second in pair_list:
        for degree in range(degrees):
            total = None
            for triple in exponents:
                if sum(triple) == degree:
                    term = weighted[first, triple] * moments[second, triple]
                    total = term if total is None else total + term
            descriptor.append(total)
    count = len(descriptor)
    padded = packed.shape[1] // 8 * per_group
    for start in range(0, padded, per_group):
        out = descriptor[min(start, count - 1)]
        for number in range(1, per_group):
            out = jnp.where(which == number, descriptor[min(start + number, count - 1)], out)
        packed[0, start * halves : start * halves + 8, :] = out
    features = jnp.concatenate(
        [packed[0, pl.ds(number, count, stride=halves), :] for number in range(halves)], axis=1
    )
    slope = linear[...] + lax.dot_general(
        matrix[...], features, (((1,), (0,)), ((), ())), precision=highest, preferred_element_type=f32
    )
    energy_out[...] = 0.5 * jnp.sum(features * (linear[...] + slope), axis=0, keepdims=True)
    for number in range(halves):
        packed[1, pl.ds(number, count, stride=halves), :] = slope[:, lanes * number : lanes * (number + 1)]

    sensitivities = []
    for number in range(count):
        sensitivities.append(
            by_half([packed[1, number * halves + h : number * halves + h + 1, :] for h in range(halves)])
        )
    backs = {}
    for triple in exponents:
        degree = sum(triple)
        for kind in range(kinds):
            total = None
            for place, (first, second) in enumerate(pair_list):
                if kind not in (first, second):
                    continue
                other = second if kind == first else first
                term = sensitivities[place * degrees + degree]
                if first == second:
                    term = term + term
                term = term * weighted[other, triple]
                total = term if total is None else total + term
            backs[kind, triple] = total

    sums = [None] * 3
    for group in range(groups):
        along = None
        tangent = [None] * 3
        for triple in exponents:
            mono = None if sum(triple) == 0 else monomials[triple][group]
            weight = None
            rise = None
            for kind in range(kinds):
                back = backs[kind, triple]
                term = slopes[group][kind] * back
                rise = term if rise is None else rise + term
                if mono is not None:
                    term = radials[group][kind] * back
                    weight = term if weight is None else weight + term
            if mono is not None:
                rise = rise * mono
            along = rise if along is None else along + rise
            if mono is None:
                continue
            for axis in range(3):
                if triple[axis] == 0:
                    continue
                lower = tuple(v - (1 if a == axis else 0) for a, v in enumerate(triple))
                term = weight if monomials[lower] is None else weight * monomials[lower][group]
                tangent[axis] = term if tangent[axis] is None else tangent[axis] + term
        direction = directions[group]
        radial_part = (
            direction[0] * tangent[0] + direction[1] * tangent[1] + direction[2] * tangent[2]
        )
        straight = along - radial_part * inverses[group]
        for axis in range(3):
            gradient = direction[axis] * straight + tangent[axis] * inverses[group]
            grads[axis, 8 * group : 8 * group + 8, :] = gradient
            sums[axis] = gradient if sums[axis] is None else sums[axis] + gradient

    items = []
    for row in range(neighbours * halves):
        value = jnp.where(
            (sub == 0) | (sub == 3),
            rows_of(grads[0, row : row + 1, :]),
            jnp.where(
                (sub == 1) | (sub == 4),
                rows_of(grads[1, row : row + 1, :]),
                rows_of(grads[2, row : row + 1, :]),
            ),
        )
        spot = spots[row : row + 1, :]
        items.append((value, spot & (lanes - 1), spot >> 7))
    product = scatter_product(items, block_count, marks[...])
    totals = [over_group(value) for value in sums]
    for number in range(own_blocks):
        self_part = jnp.concatenate([totals[axis][number : number + 1] for axis in range(3)], axis=0)
        own_out[:, lanes * number : lanes * (number + 1)] = summed(product, number) - self_part
    trans_out[...] = summed(product, own_blocks)
    first_out[...] = summed(product, own_blocks + 1)
    second_out[...] = summed(product, own_blocks + 2)


def shock_back_kernel(own, trans, back_first, back_second, shock_spots, own_out, trans_out):
    own_blocks = own.shape[1] // lanes
    width = trans_out.shape[2]
    items = []
    for way, back in enumerate((back_first, back_second)):
        spot = shock_spots[way : way + 1, :]
        items.append((twice(back[...]), spot & (lanes - 1), spot >> 7))
    product = scatter_product(items, own_blocks + 1)
    for number in range(own_blocks):
        cut = slice(lanes * number, lanes * (number + 1))
        own_out[:, cut] = own[:, cut] + summed(product, number)
    ghosts = trans[...] + summed(product, own_blocks)
    trans_out[0] = ghosts[:, :width]
    trans_out[1] = ghosts[:, width : 2 * width]


def force_kernel(half_velocity, displaced, own, back, trans_spots, leaving_spots, force_out, payload_out):
    own_blocks = own.shape[1] // lanes
    items = []
    for way in range(2):
        spot = trans_spots[way : way + 1, :]
        items.append((twice(pad_lanes(back[1 - way])), spot & (lanes - 1), spot >> 7))
    product = scatter_product(items, own_blocks)
    leaving = payload_out.shape[2]
    blocks = []
    for number in range(own_blocks):
        cut = slice(lanes * number, lanes * (number + 1))
        new_force = -(own[:, cut] + summed(product, number))
        force_out[:, cut] = new_force
        new_velocity = half_velocity[:, cut] + kick_factor * new_force
        blocks.append(
            jnp.concatenate(
                [pad_rows(displaced[:, cut]), pad_rows(new_velocity), pad_rows(new_force)], axis=0
            )
        )
    picked = pick_columns(blocks, leaving_spots[...])
    for number in range(3):
        payload_out[number] = picked[8 * number : 8 * number + 3, :leaving]


def write_kernel(half_velocity, kept, displaced, new_force, energy, disp_out, vel_out, force_out, energy_out):
    keep = kept[...]
    force = new_force[...]
    disp_out[...] = displaced[...] * keep
    vel_out[...] = (half_velocity[...] + kick_factor * force) * keep
    force_out[...] = force * keep
    energy_out[...] = energy[...] * keep


def along_shock(x, by):
    devices = lax.axis_size("shock")
    return lax.ppermute(
        x, "shock", [(i, i + by) for i in range(devices) if 0 <= i + by < devices]
    )


def with_partner(x, start):
    devices = lax.axis_size("shock")
    lows = range(start, devices - 1, 2)
    return lax.ppermute(x, "shock", [(i, i + 1) for i in lows] + [(i + 1, i) for i in lows])


def across(x):
    devices = lax.axis_size("trans")
    down = [(i, (i - 1) % devices) for i in range(devices)]
    up = [(i, (i + 1) % devices) for i in range(devices)]
    if sorted(down) == sorted(up):
        return lax.ppermute(x, "trans", down)
    return jnp.stack([lax.ppermute(x[0], "trans", down), lax.ppermute(x[1], "trans", up)])


def shaped(*dims, kind=f32):
    return pltpu.VMEM(dims, kind)


def run_kernel(kernel, out_shape, args, scratch=(), far=0, cost=None):
    vmem = pl.BlockSpec(memory_space=pltpu.VMEM)
    args = [
        arg if place < far else pltpu.with_memory_space_constraint(arg, pltpu.VMEM)
        for place, arg in enumerate(args)
    ]
    return pl.pallas_call(
        kernel,
        in_specs=[vmem] * len(args),
        out_specs=tuple(vmem for _ in out_shape),
        out_shape=out_shape,
        scratch_shapes=list(scratch),
        cost_estimate=cost,
    )(*args)


def shards(
    displacement,
    velocity,
    force_before,
    beta,
    alpha,
    live_count,
    trans_send,
    shock_send,
    neighbour_block,
    neighbour_lane,
    leaving_slots,
    leaving_count,
):
    slots = displacement.shape[1]
    trans_width = trans_send.shape[1]
    shock_width = shock_send.shape[1]
    neighbours = neighbour_block.shape[0]
    leaving = leaving_slots.shape[0]
    halves = slots // lanes
    groups = -(-neighbours // (8 // halves))
    count = len(pair_list) * degrees
    assert slots % lanes == 0 and 8 % halves == 0 and halves <= 4
    assert shock_width == lanes and 2 * trans_width <= lanes
    displaced, trans_go = run_kernel(
        start_kernel,
        (shaped(3, slots), shaped(2, 3, trans_width)),
        (displacement, velocity, force_before, trans_send),
        far=4,
    )
    trans_in = across(trans_go)
    whole = jnp.int32
    shock_spots, spots, linear, matrix = run_kernel(
        prepare_kernel,
        (
            shaped(2, shock_width, kind=whole),
            shaped(groups * 8, lanes, kind=whole),
            shaped(count, slots),
            shaped(count, count),
        ),
        (shock_send, neighbour_block, neighbour_lane, beta.reshape(1, count), alpha, trans_go),
        far=5,
        cost=pl.CostEstimate(flops=40 * slots * neighbours, bytes_accessed=12 * slots * neighbours, transcendentals=0),
    )
    to_first, to_second = run_kernel(
        shock_kernel,
        (shaped(3, shock_width), shaped(3, shock_width)),
        (displaced, trans_in, shock_spots),
        (pltpu.VMEM((8, lanes), f32),),
    )
    from_second = with_partner(to_second, 1)
    from_first = with_partner(to_first, 0)
    (marks,) = run_kernel(
        mark_kernel,
        (shaped(lanes, neighbours * slots, kind=bf16),),
        (spots,),
        cost=pl.CostEstimate(
            flops=2 * lanes * neighbours * slots, bytes_accessed=2 * lanes * neighbours * slots, transcendentals=0
        ),
    )
    packed_rows = -(-(count * halves) // 8) * 8
    energy, own, trans, first, second = run_kernel(
        energy_kernel,
        (shaped(1, slots), shaped(3, slots), shaped(3, lanes), shaped(3, lanes), shaped(3, lanes)),
        (displaced, trans_in, from_first, from_second, spots, linear, matrix, marks),
        (
            pltpu.VMEM((8, lanes), f32),
            pltpu.VMEM((3, groups * 8, lanes), f32),
            pltpu.VMEM((2, packed_rows, lanes), f32),
        ),
    )
    back_second = with_partner(second, 1)
    back_first = with_partner(first, 0)
    half_velocity, kept, trans_spots, leaving_spots = run_kernel(
        settle_kernel,
        (
            shaped(3, slots),
            shaped(1, slots),
            shaped(2, lanes, kind=whole),
            shaped(1, lanes, kind=whole),
        ),
        (
            jnp.concatenate([live_count, leaving_count]).reshape(1, 2),
            velocity,
            force_before,
            trans_send,
            leaving_slots.reshape(1, leaving),
            own,
        ),
        far=5,
        cost=pl.CostEstimate(flops=40 * slots, bytes_accessed=400 * slots, transcendentals=0),
    )
    own, trans_go = run_kernel(
        shock_back_kernel,
        (shaped(3, slots), shaped(2, 3, trans_width)),
        (own, trans, back_first, back_second, shock_spots),
    )
    back = across(trans_go)
    new_force, payload = run_kernel(
        force_kernel,
        (shaped(3, slots), shaped(3, 3, leaving)),
        (half_velocity, displaced, own, back, trans_spots, leaving_spots),
    )
    wide = jax.ShapeDtypeStruct((3, slots), f32)
    disp_next, vel_next, force_next, energy = run_kernel(
        write_kernel,
        (wide, wide, wide, jax.ShapeDtypeStruct((1, slots), f32)),
        (half_velocity, kept, displaced, new_force, energy),
        cost=pl.CostEstimate(flops=9 * slots, bytes_accessed=80 * slots, transcendentals=0),
    )
    arrivals = along_shock(payload, -1)
    return (disp_next, vel_next, force_next, energy.reshape(slots), arrivals)


def solution(mesh):
    both = ("shock", "trans")
    in_specs = (
        P(None, both),
        P(None, both),
        P(None, both),
        P(),
        P(),
        P(both),
        P(None, both),
        P(None, both),
        P(None, both),
        P(None, both),
        P(both),
        P(both),
    )
    out_specs = (P(None, both), P(None, both), P(None, both), P(both), P(None, None, both))
    return jax.shard_map(shards, mesh=mesh, in_specs=in_specs, out_specs=out_specs, check_vma=False)
```

profile of v0, /device:TPU:11, one launch (start us, length us, event | category | flops | bytes accessed | tf_op | source)
XLA Modules:
  0.0 29.3 jit_solution(3523436565721790270)
XLA Ops:
  0.6 0.8 %shard_map.155 = (f32[3,256]{1,0:T(4,128)S(1)}, f32[2,3,32]{2,1,0:T(4,128)S(1)}) custom-call(f32[3,256]{1,0:T(4,128)} %disp.1, f32[3,256]{1,0:T(4,128)} %vel.3, f32[3,256]{1,0:T(4,128)} %force.3, s32[2,32]{1,0:T(2,128)} %trans_send.3), custom_call_target="tpu_custom_call" | custom-call | tf_op jit(solution)/shard_map/pallas_call | solution.py:564
  1.4 1.2 %collective-permute-start = (f32[2,3,32]{2,1,0:T(4,128)S(1)}, f32[2,3,32]{2,1,0:T(4,128)S(1)}, u32[]{:S(2)}, u32[]{:S(2)}) collective-permute-start(f32[2,3,32]{2,1,0:T(4,128)S(1)} %get-tuple-element.31.trans_like), channel_id=1, source_target_pairs={{0,1},{1,0},{2,3},{3,2},{4,5},{5,4},{6,7},{7,6},{8,9},{9,8},{10,11... | collective-permute-start | bytes 2312 | tf_op jit(solution)/shard_map/ppermute | solution.py:550
  2.7 0.9 %shard_map.156 = (s32[2,128]{1,0:T(2,128)S(1)}, s32[56,128]{1,0:T(8,128)S(1)}, f32[50,256]{1,0:T(8,128)S(1)}, f32[50,50]{1,0:T(8,128)S(1)}) custom-call(s32[2,128]{1,0:T(2,128)} %shock_send.1, s32[26,256]{1,0:T(8,128)} %neighbour_block.1, s32[26,256]{1,0:T(8,128)} %neighbour_lane.1, f32[1,50]{1,0:T(1,128)} %bitcast.5, f32[50,50]{1,0:T(8,128)} %alpha.1, ...), custom_call_target="tpu_custom_call" | custom-call | flops 266240 | bytes 79872 | tf_op jit(solution)/shard_map/pallas_call | solution.py:564
  3.6 0.3 collective-permute-done.trans_in
  3.9 0.1 shard_map.157
  4.0 1.8 %collective-permute-start.1 = (f32[3,128]{1,0:T(4,128)S(1)}, f32[3,128]{1,0:T(4,128)S(1)}, u32[]{:S(2)}, u32[]{:S(2)}) collective-permute-start(f32[3,128]{1,0:T(4,128)S(1)} %get-tuple-element.33), channel_id=1, source_target_pairs={{0,2},{4,6},{8,10},{12,14},{16,18},{20,22},{24,26},{28,30},{2,0},{... | collective-permute-start | bytes 4616 | tf_op jit(solution)/shard_map/ppermute | solution.py:542
  5.9 3.1 %collective-permute-start.2 = (f32[3,128]{1,0:T(4,128)S(1)}, f32[3,128]{1,0:T(4,128)S(1)}, u32[]{:S(2)}, u32[]{:S(2)}) collective-permute-start(f32[3,128]{1,0:T(4,128)S(1)} %get-tuple-element.34), channel_id=1, source_target_pairs={{2,4},{6,8},{10,12},{14,16},{18,20},{22,24},{26,28},{4,2},{8,6},{1... | collective-permute-start | bytes 4616 | tf_op jit(solution)/shard_map/ppermute | solution.py:542
  8.9 0.4 %shard_map.158.marks = bf16[128,6656]{1,0:T(8,128)(2,1)S(1)} custom-call(s32[56,128]{1,0:T(8,128)S(1)} %get-tuple-element.35.spots), custom_call_target="tpu_custom_call" | custom-call | flops 1703936 | bytes 1703936 | tf_op jit(solution)/shard_map/pallas_call | solution.py:564
  9.3 0.0 collective-permute-done.1.from_first
  9.3 2.4 %collective-permute-done.2.from_second = f32[3,128]{1,0:T(4,128)S(1)} collective-permute-done((f32[3,128]{1,0:T(4,128)S(1)}, f32[3,128]{1,0:T(4,128)S(1)}, u32[]{:S(2)}, u32[]{:S(2)}) %collective-permute-start.2) | collective-permute-done | bytes 1568 | tf_op jit(solution)/shard_map/ppermute | solution.py:542
  11.7 2.1 %shard_map.159 = (f32[1,256]{1,0:T(1,128)S(1)}, f32[3,256]{1,0:T(4,128)S(1)}, f32[3,128]{1,0:T(4,128)S(1)}, f32[3,128]{1,0:T(4,128)S(1)}, f32[3,128]{1,0:T(4,128)S(1)}) custom-call(f32[3,256]{1,0:T(4,128)S(1)} %get-tuple-element.30.displaced, f32[2,3,32]{2,1,0:T(4,128)S(1)} %collective-permute-done.trans_in, f32[3,128]{1,0:T(4,128)S(1)} %collective-permute-done.1.from_first, ...), custom_call_target="tpu_custom_call" | custom-call | tf_op jit(solution)/shard_map/pallas_call | solution.py:564
  13.8 0.1 collective-permute-start.3
  13.9 3.1 %collective-permute-start.4 = (f32[3,128]{1,0:T(4,128)S(1)}, f32[3,128]{1,0:T(4,128)S(1)}, u32[]{:S(2)}, u32[]{:S(2)}) collective-permute-start(f32[3,128]{1,0:T(4,128)S(1)} %get-tuple-element.43), channel_id=1, source_target_pairs={{2,4},{6,8},{10,12},{14,16},{18,20},{22,24},{26,28},{4,2},{8,6},{1... | collective-permute-start | bytes 4616 | tf_op jit(solution)/shard_map/ppermute | solution.py:542
  18.3 0.0 collective-permute-done.3.back_first
  18.3 1.4 %collective-permute-done.4.back_second = f32[3,128]{1,0:T(4,128)S(1)} collective-permute-done((f32[3,128]{1,0:T(4,128)S(1)}, f32[3,128]{1,0:T(4,128)S(1)}, u32[]{:S(2)}, u32[]{:S(2)}) %collective-permute-start.4) | collective-permute-done | bytes 1568 | tf_op jit(solution)/shard_map/ppermute | solution.py:542
  19.7 0.2 shard_map.161
  19.9 1.3 %collective-permute-start.5 = (f32[2,3,32]{2,1,0:T(4,128)S(1)}, f32[2,3,32]{2,1,0:T(4,128)S(1)}, u32[]{:S(2)}, u32[]{:S(2)}) collective-permute-start(f32[2,3,32]{2,1,0:T(4,128)S(1)} %get-tuple-element.45), channel_id=1, source_target_pairs={{0,1},{1,0},{2,3},{3,2},{4,5},{5,4},{6,7},{7,6},{8,9},{9,8},{10,11... | collective-permute-start | bytes 2312 | tf_op jit(solution)/shard_map/ppermute | solution.py:550
  21.2 0.6 %add_bitcast_fusion.counts = s32[1,2]{1,0:T(1,128)} fusion(s32[1]{0:T(128)S(6)} %copy.19, s32[1]{0:T(128)S(6)} %copy.18), kind=kLoop, calls=%fused_computation | loop fusion | flops 2 | bytes 16 | tf_op jit(solution)/shard_map/reshape | solution.py:656
  21.8 0.9 %shard_map.160 = (f32[3,256]{1,0:T(4,128)S(1)}, f32[1,256]{1,0:T(1,128)S(1)}, s32[2,128]{1,0:T(2,128)S(1)}, s32[1,128]{1,0:T(1,128)S(1)}) custom-call(s32[1,2]{1,0:T(1,128)} %add_bitcast_fusion.counts, f32[3,256]{1,0:T(4,128)} %vel.3, f32[3,256]{1,0:T(4,128)} %force.3, s32[2,32]{1,0:T(2,128)} %trans_send.3, s32[1,16]{1,0:T(1,128)} %bitcast.6, ...), custom_call_target="tpu_custom_call" | custom-call | flops 10240 | bytes 102400 | tf_op jit(solution)/shard_map/pallas_call | solution.py:564
  22.7 0.0 collective-permute-done.5.back
  22.7 0.2 shard_map.162
  22.9 2.4 %collective-permute-start.6 = (f32[3,3,16]{2,1,0:T(4,128)S(1)}, f32[3,3,16]{2,1,0:T(4,128)S(1)}, u32[]{:S(2)}, u32[]{:S(2)}) collective-permute-start(f32[3,3,16]{2,1,0:T(4,128)S(1)} %get-tuple-element.54), channel_id=1, source_target_pairs={{2,0},{4,2},{6,4},{8,6},{10,8},{12,10},{14,12},{16,14},{18,16},{20... | collective-permute-start | bytes 1736 | tf_op jit(solution)/shard_map/ppermute | solution.py:534
  25.3 0.6 %shard_map.163 = (f32[3,256]{1,0:T(4,128)}, f32[3,256]{1,0:T(4,128)}, f32[3,256]{1,0:T(4,128)}, f32[1,256]{1,0:T(1,128)}) custom-call(f32[3,256]{1,0:T(4,128)S(1)} %get-tuple-element.39.half_velocity, f32[1,256]{1,0:T(1,128)S(1)} %get-tuple-element.40.kept, f32[3,256]{1,0:T(4,128)S(1)} %get-tuple-element.30.displaced, ...), custom_call_target="tpu_custom_call" | custom-call | flops 2304 | bytes 20480 | tf_op jit(solution)/shard_map/pallas_call | solution.py:564
  25.9 2.9 %collective-permute-done.6 = f32[3,3,16]{2,1,0:T(4,128)S(1)} collective-permute-done((f32[3,3,16]{2,1,0:T(4,128)S(1)}, f32[3,3,16]{2,1,0:T(4,128)S(1)}, u32[]{:S(2)}, u32[]{:S(2)}) %collective-permute-start.6) | collective-permute-done | bytes 608 | tf_op jit(solution)/shard_map/ppermute | solution.py:534
  28.7 0.6 %copy.20 = f32[3,3,16]{2,1,0:T(4,128)} copy(f32[3,3,16]{2,1,0:T(4,128)S(1)} %collective-permute-done.6) | data formatting | bytes 1152
Async XLA Ops:
  1.4 2.5 %collective-permute-start = (f32[2,3,32]{2,1,0:T(4,128)S(1)}, f32[2,3,32]{2,1,0:T(4,128)S(1)}, u32[]{:S(2)}, u32[]{:S(2)}) collective-permute-start(f32[2,3,32]{2,1,0:T(4,128)S(1)} %get-tuple-element.31.trans_like), channel_id=1, source_target_pairs={{0,1},{1,0},{2,3},{3,2},{4,5},{5,4},{6,7},{7,6},{8,9},{9,8},{10,11... | collective-permute-start | bytes 2312 | tf_op jit(solution)/shard_map/ppermute | solution.py:550
  4.0 5.3 %collective-permute-start.1 = (f32[3,128]{1,0:T(4,128)S(1)}, f32[3,128]{1,0:T(4,128)S(1)}, u32[]{:S(2)}, u32[]{:S(2)}) collective-permute-start(f32[3,128]{1,0:T(4,128)S(1)} %get-tuple-element.33), channel_id=1, source_target_pairs={{0,2},{4,6},{8,10},{12,14},{16,18},{20,22},{24,26},{28,30},{2,0},{... | collective-permute-start | bytes 4616 | tf_op jit(solution)/shard_map/ppermute | solution.py:542
  5.9 5.8 %collective-permute-start.2 = (f32[3,128]{1,0:T(4,128)S(1)}, f32[3,128]{1,0:T(4,128)S(1)}, u32[]{:S(2)}, u32[]{:S(2)}) collective-permute-start(f32[3,128]{1,0:T(4,128)S(1)} %get-tuple-element.34), channel_id=1, source_target_pairs={{2,4},{6,8},{10,12},{14,16},{18,20},{22,24},{26,28},{4,2},{8,6},{1... | collective-permute-start | bytes 4616 | tf_op jit(solution)/shard_map/ppermute | solution.py:542
  13.8 4.4 %collective-permute-start.3 = (f32[3,128]{1,0:T(4,128)S(1)}, f32[3,128]{1,0:T(4,128)S(1)}, u32[]{:S(2)}, u32[]{:S(2)}) collective-permute-start(f32[3,128]{1,0:T(4,128)S(1)} %get-tuple-element.42), channel_id=1, source_target_pairs={{0,2},{4,6},{8,10},{12,14},{16,18},{20,22},{24,26},{28,30},{2,0},{... | collective-permute-start | bytes 4616 | tf_op jit(solution)/shard_map/ppermute | solution.py:542
  13.9 5.8 %collective-permute-start.4 = (f32[3,128]{1,0:T(4,128)S(1)}, f32[3,128]{1,0:T(4,128)S(1)}, u32[]{:S(2)}, u32[]{:S(2)}) collective-permute-start(f32[3,128]{1,0:T(4,128)S(1)} %get-tuple-element.43), channel_id=1, source_target_pairs={{2,4},{6,8},{10,12},{14,16},{18,20},{22,24},{26,28},{4,2},{8,6},{1... | collective-permute-start | bytes 4616 | tf_op jit(solution)/shard_map/ppermute | solution.py:542
  19.9 2.7 %collective-permute-start.5 = (f32[2,3,32]{2,1,0:T(4,128)S(1)}, f32[2,3,32]{2,1,0:T(4,128)S(1)}, u32[]{:S(2)}, u32[]{:S(2)}) collective-permute-start(f32[2,3,32]{2,1,0:T(4,128)S(1)} %get-tuple-element.45), channel_id=1, source_target_pairs={{0,1},{1,0},{2,3},{3,2},{4,5},{5,4},{6,7},{7,6},{8,9},{9,8},{10,11... | collective-permute-start | bytes 2312 | tf_op jit(solution)/shard_map/ppermute | solution.py:550
  22.9 5.9 %collective-permute-start.6 = (f32[3,3,16]{2,1,0:T(4,128)S(1)}, f32[3,3,16]{2,1,0:T(4,128)S(1)}, u32[]{:S(2)}, u32[]{:S(2)}) collective-permute-start(f32[3,3,16]{2,1,0:T(4,128)S(1)} %get-tuple-element.54), channel_id=1, source_target_pairs={{2,0},{4,2},{6,4},{8,6},{10,8},{12,10},{14,12},{16,14},{18,16},{20... | collective-permute-start | bytes 1736 | tf_op jit(solution)/shard_map/ppermute | solution.py:534
where the time goes:
time: 29.7 us; the launch traced here: 29.3 us
  starting transfers between devices  12.9 us (43%)
  waiting for transfers between devices  6.92 us (23%)
  Pallas kernels  6.3 us (21%)
  between operations  2.04 us (7%)
  local copies, waits for them, and re-layouts  0.59 us (2%)
  other arithmetic  0.58 us (2%)
    ppermute x4, starting transfers between devices, with_partner(): lax.ppermute(x, 'shock', [(i, i + 1) for i in lows] + [(i + 1, i) for i i...  8.02 us
    pallas_call x9, Pallas kernels, run_kernel(): pl.pallas_call(kernel, in_specs=[vmem] * len(args), out_specs=tuple((vmem...  6.3 us
    ppermute x4, waiting for transfers between devices, with_partner(): lax.ppermute(x, 'shock', [(i, i + 1) for i in lows] + [(i + 1, i) for i i...  3.78 us
    ppermute x1, waiting for transfers between devices, along_shock(): lax.ppermute(x, 'shock', [(i, i + by) for i in range(devices) if 0 <= i +...  2.86 us
    ppermute x2, starting transfers between devices, across(): return lax.ppermute(x, 'trans', down)  2.5 us
    ppermute x1, starting transfers between devices, along_shock(): lax.ppermute(x, 'shock', [(i, i + by) for i in range(devices) if 0 <= i +...  2.37 us
  transfers between devices with their start and end apart: 7, of which 4 were waited for; matrix products, arithmetic and copies ran while one was open for 2% of the time, Pallas kernels for 10%

commit v1 on v0

--- a/solution.py
+++ b/solution.py
@@ -175,14 +175,14 @@
 
 
 def settle_kernel(
-    counts,
     vel,
     force,
     trans_send,
     leaving_slots,
+    count_row,
     after,
     half_out,
-    kept_out,
+    stay_out,
     trans_spots_out,
     leaving_out,
 ):
@@ -191,7 +191,7 @@
     trans_spots_out[...] = pad_lanes(trans_send[...], -1)
     leaving = leaving_slots.shape[1]
     entry = lax.broadcasted_iota(jnp.int32, (1, leaving), 1)
-    going = jnp.where(entry < jnp.broadcast_to(counts[:, 1:2], (1, leaving)), leaving_slots[...], -1)
+    going = jnp.where(entry < count_row[:, :leaving], leaving_slots[...], -1)
     leaving_out[...] = pad_lanes(going, -1)
     square = (leaving, leaving)
     eye = lax.broadcasted_iota(jnp.int32, square, 0) == lax.broadcasted_iota(jnp.int32, square, 1)
@@ -201,8 +201,11 @@
     slot = lax.broadcasted_iota(jnp.int32, (leaving, slots), 1)
     gone = jnp.where(slot.astype(f32) == jnp.broadcast_to(upright, slot.shape), 1.0, 0.0)
     gone = jnp.sum(gone, axis=0, keepdims=True)
-    live = slot[:1] < jnp.broadcast_to(counts[:, 0:1], (1, slots))
-    kept_out[...] = jnp.where(live, 1.0 - gone, 0.0)
+    stay_out[...] = 1.0 - gone
+
+
+def tally_kernel(leaving_count, count_out):
+    count_out[...] = jnp.broadcast_to(leaving_count[...].reshape(1, 1), (1, lanes))
 
 
 def mark_kernel(spots, marks_out):
@@ -520,8 +523,12 @@
         payload_out[number] = picked[8 * number : 8 * number + 3, :leaving]
 
 
-def write_kernel(half_velocity, kept, displaced, new_force, energy, disp_out, vel_out, force_out, energy_out):
-    keep = kept[...]
+def write_kernel(
+    live_count, half_velocity, stay, displaced, new_force, energy, disp_out, vel_out, force_out, energy_out
+):
+    slot = lax.broadcasted_iota(jnp.int32, stay.shape, 1)
+    live = slot < jnp.broadcast_to(live_count[...].reshape(1, 1), stay.shape)
+    keep = jnp.where(live, stay[...], 0.0)
     force = new_force[...]
     disp_out[...] = displaced[...] * keep
     vel_out[...] = (half_velocity[...] + kick_factor * force) * keep
@@ -623,6 +630,7 @@
     )
     from_second = with_partner(to_second, 1)
     from_first = with_partner(to_first, 0)
+    (count_row,) = run_kernel(tally_kernel, (shaped(1, lanes, kind=whole),), (leaving_count,), far=1)
     (marks,) = run_kernel(
         mark_kernel,
         (shaped(lanes, neighbours * slots, kind=bf16),),
@@ -644,7 +652,7 @@
     )
     back_second = with_partner(second, 1)
     back_first = with_partner(first, 0)
-    half_velocity, kept, trans_spots, leaving_spots = run_kernel(
+    half_velocity, stay, trans_spots, leaving_spots = run_kernel(
         settle_kernel,
         (
             shaped(3, slots),
@@ -653,14 +661,14 @@
             shaped(1, lanes, kind=whole),
         ),
         (
-            jnp.concatenate([live_count, leaving_count]).reshape(1, 2),
             velocity,
             force_before,
             trans_send,
             leaving_slots.reshape(1, leaving),
+            count_row,
             own,
         ),
-        far=5,
+        far=4,
         cost=pl.CostEstimate(flops=40 * slots, bytes_accessed=400 * slots, transcendentals=0),
     )
     own, trans_go = run_kernel(
@@ -678,7 +686,8 @@
     disp_next, vel_next, force_next, energy = run_kernel(
         write_kernel,
         (wide, wide, wide, jax.ShapeDtypeStruct((1, slots), f32)),
-        (half_velocity, kept, displaced, new_force, energy),
+        (live_count, half_velocity, stay, displaced, new_force, energy),
+        far=1,
         cost=pl.CostEstimate(flops=9 * slots, bytes_accessed=80 * slots, transcendentals=0),
     )
     arrivals = along_shock(payload, -1)

time: 29.7 us -> 29.7 us (level)
  waiting for transfers between devices: 6.92 us -> 7.55 us
  other arithmetic: 0.58 us -> 0 us
    ppermute x4, waiting for transfers between devices: 3.78 us -> 5.08 us  [with_partner(): lax.ppermute(x, 'shock', [(i, i + 1) for i in lows] + [(i + 1, i) for i i...]
    ppermute x1, waiting for transfers between devices: 2.86 us -> 2.19 us  [along_shock(): lax.ppermute(x, 'shock', [(i, i + by) for i in range(devices) if 0 <= i +...]
    reshape x1 -> x0, other arithmetic: 0.58 us -> none  [shards(): jnp.concatenate([live_count, leaving_count]).reshape(1, 2)]
    pallas_call x9 -> x10, Pallas kernels: 6.3 us -> 6.37 us  [run_kernel(): pl.pallas_call(kernel, in_specs=[vmem] * len(args), out_specs=tuple((vmem...]
  transfers between devices with their start and end apart: 7 -> 7, of which waited for: 4 -> 4; matrix products, arithmetic and copies ran while one was open for 2% -> 0% of each run, Pallas kernels for 10% -> 10%
where the time goes in v1:
time: 29.7 us; the launch traced here: 29.4 us
  starting transfers between devices  12.8 us (43%)
  waiting for transfers between devices  7.55 us (25%)
  Pallas kernels  6.37 us (21%)
  between operations  2.04 us (7%)
  local copies, waits for them, and re-layouts  0.59 us (2%)
    ppermute x4, starting transfers between devices, with_partner(): lax.ppermute(x, 'shock', [(i, i + 1) for i in lows] + [(i + 1, i) for i i...  8.02 us
    pallas_call x10, Pallas kernels, run_kernel(): pl.pallas_call(kernel, in_specs=[vmem] * len(args), out_specs=tuple((vmem...  6.37 us
    ppermute x4, waiting for transfers between devices, with_partner(): lax.ppermute(x, 'shock', [(i, i + 1) for i in lows] + [(i + 1, i) for i i...  5.08 us
    ppermute x2, starting transfers between devices, across(): return lax.ppermute(x, 'trans', down)  2.5 us
    ppermute x1, starting transfers between devices, along_shock(): lax.ppermute(x, 'shock', [(i, i + by) for i in range(devices) if 0 <= i +...  2.32 us
    ppermute x1, waiting for transfers between devices, along_shock(): lax.ppermute(x, 'shock', [(i, i + by) for i in range(devices) if 0 <= i +...  2.19 us
  transfers between devices with their start and end apart: 7, of which 4 were waited for; matrix products, arithmetic and copies ran while one was open for 0% of the time, Pallas kernels for 10%

profile of v1, /device:TPU:11, one launch (start us, length us, event | category | flops | bytes accessed | tf_op | source)
XLA Modules:
  0.0 29.4 jit_solution(357317870704342385)
XLA Ops:
  0.6 0.8 %shard_map.156 = (f32[3,256]{1,0:T(4,128)S(1)}, f32[2,3,32]{2,1,0:T(4,128)S(1)}) custom-call(f32[3,256]{1,0:T(4,128)} %disp.1, f32[3,256]{1,0:T(4,128)} %vel.3, f32[3,256]{1,0:T(4,128)} %force.3, s32[2,32]{1,0:T(2,128)} %trans_send.3), custom_call_target="tpu_custom_call" | custom-call | tf_op jit(solution)/shard_map/pallas_call | solution.py:571
  1.4 1.2 %collective-permute-start = (f32[2,3,32]{2,1,0:T(4,128)S(1)}, f32[2,3,32]{2,1,0:T(4,128)S(1)}, u32[]{:S(2)}, u32[]{:S(2)}) collective-permute-start(f32[2,3,32]{2,1,0:T(4,128)S(1)} %get-tuple-element.31.trans_like), channel_id=1, source_target_pairs={{0,1},{1,0},{2,3},{3,2},{4,5},{5,4},{6,7},{7,6},{8,9},{9,8},{10,11... | collective-permute-start | bytes 2312 | tf_op jit(solution)/shard_map/ppermute | solution.py:557
  2.7 0.9 %shard_map.157 = (s32[2,128]{1,0:T(2,128)S(1)}, s32[56,128]{1,0:T(8,128)S(1)}, f32[50,256]{1,0:T(8,128)S(1)}, f32[50,50]{1,0:T(8,128)S(1)}) custom-call(s32[2,128]{1,0:T(2,128)} %shock_send.1, s32[26,256]{1,0:T(8,128)} %neighbour_block.1, s32[26,256]{1,0:T(8,128)} %neighbour_lane.1, f32[1,50]{1,0:T(1,128)} %bitcast.3, f32[50,50]{1,0:T(8,128)} %alpha.1, ...), custom_call_target="tpu_custom_call" | custom-call | flops 266240 | bytes 79872 | tf_op jit(solution)/shard_map/pallas_call | solution.py:571
  3.6 0.3 collective-permute-done.trans_in
  3.9 0.1 shard_map.158
  4.0 1.8 %collective-permute-start.1 = (f32[3,128]{1,0:T(4,128)S(1)}, f32[3,128]{1,0:T(4,128)S(1)}, u32[]{:S(2)}, u32[]{:S(2)}) collective-permute-start(f32[3,128]{1,0:T(4,128)S(1)} %get-tuple-element.33), channel_id=1, source_target_pairs={{0,2},{4,6},{8,10},{12,14},{16,18},{20,22},{24,26},{28,30},{2,0},{... | collective-permute-start | bytes 4616 | tf_op jit(solution)/shard_map/ppermute | solution.py:549
  5.9 3.1 %collective-permute-start.2 = (f32[3,128]{1,0:T(4,128)S(1)}, f32[3,128]{1,0:T(4,128)S(1)}, u32[]{:S(2)}, u32[]{:S(2)}) collective-permute-start(f32[3,128]{1,0:T(4,128)S(1)} %get-tuple-element.34), channel_id=1, source_target_pairs={{2,4},{6,8},{10,12},{14,16},{18,20},{22,24},{26,28},{4,2},{8,6},{1... | collective-permute-start | bytes 4616 | tf_op jit(solution)/shard_map/ppermute | solution.py:549
  8.9 0.4 %shard_map.159.marks = bf16[128,6656]{1,0:T(8,128)(2,1)S(1)} custom-call(s32[56,128]{1,0:T(8,128)S(1)} %get-tuple-element.35.spots), custom_call_target="tpu_custom_call" | custom-call | flops 1703936 | bytes 1703936 | tf_op jit(solution)/shard_map/pallas_call | solution.py:571
  9.3 0.0 collective-permute-done.1.from_first
  9.3 2.4 %collective-permute-done.2.from_second = f32[3,128]{1,0:T(4,128)S(1)} collective-permute-done((f32[3,128]{1,0:T(4,128)S(1)}, f32[3,128]{1,0:T(4,128)S(1)}, u32[]{:S(2)}, u32[]{:S(2)}) %collective-permute-start.2) | collective-permute-done | bytes 1568 | tf_op jit(solution)/shard_map/ppermute | solution.py:549
  11.7 2.1 %shard_map.160 = (f32[1,256]{1,0:T(1,128)S(1)}, f32[3,256]{1,0:T(4,128)S(1)}, f32[3,128]{1,0:T(4,128)S(1)}, f32[3,128]{1,0:T(4,128)S(1)}, f32[3,128]{1,0:T(4,128)S(1)}) custom-call(f32[3,256]{1,0:T(4,128)S(1)} %get-tuple-element.30.displaced, f32[2,3,32]{2,1,0:T(4,128)S(1)} %collective-permute-done.trans_in, f32[3,128]{1,0:T(4,128)S(1)} %collective-permute-done.1.from_first, ...), custom_call_target="tpu_custom_call" | custom-call | tf_op jit(solution)/shard_map/pallas_call | solution.py:571
  13.8 0.1 collective-permute-start.3
  13.9 3.1 %collective-permute-start.4 = (f32[3,128]{1,0:T(4,128)S(1)}, f32[3,128]{1,0:T(4,128)S(1)}, u32[]{:S(2)}, u32[]{:S(2)}) collective-permute-start(f32[3,128]{1,0:T(4,128)S(1)} %get-tuple-element.43), channel_id=1, source_target_pairs={{2,4},{6,8},{10,12},{14,16},{18,20},{22,24},{26,28},{4,2},{8,6},{1... | collective-permute-start | bytes 4616 | tf_op jit(solution)/shard_map/ppermute | solution.py:549
  17.0 0.0 collective-permute-done.3.back_first
  17.0 2.7 %collective-permute-done.4.back_second = f32[3,128]{1,0:T(4,128)S(1)} collective-permute-done((f32[3,128]{1,0:T(4,128)S(1)}, f32[3,128]{1,0:T(4,128)S(1)}, u32[]{:S(2)}, u32[]{:S(2)}) %collective-permute-start.4) | collective-permute-done | bytes 1568 | tf_op jit(solution)/shard_map/ppermute | solution.py:549
  19.7 0.2 shard_map.162
  19.9 1.3 %collective-permute-start.5 = (f32[2,3,32]{2,1,0:T(4,128)S(1)}, f32[2,3,32]{2,1,0:T(4,128)S(1)}, u32[]{:S(2)}, u32[]{:S(2)}) collective-permute-start(f32[2,3,32]{2,1,0:T(4,128)S(1)} %get-tuple-element.45), channel_id=1, source_target_pairs={{0,1},{1,0},{2,3},{3,2},{4,5},{5,4},{6,7},{7,6},{8,9},{9,8},{10,11... | collective-permute-start | bytes 2312 | tf_op jit(solution)/shard_map/ppermute | solution.py:557
  21.8 0.1 shard_map.155.count_row
  21.9 0.8 %shard_map.161 = (f32[3,256]{1,0:T(4,128)S(1)}, f32[1,256]{1,0:T(1,128)S(1)}, s32[2,128]{1,0:T(2,128)S(1)}, s32[1,128]{1,0:T(1,128)S(1)}) custom-call(f32[3,256]{1,0:T(4,128)} %vel.3, f32[3,256]{1,0:T(4,128)} %force.3, s32[2,32]{1,0:T(2,128)} %trans_send.3, s32[1,16]{1,0:T(1,128)} %bitcast.4, s32[1,128]{1,0:T(1,128)S(1)} %shard_map.155.count_row, ...), custom_call_target="tpu_custom_call" | custom-call | flops 10240 | bytes 102400 | tf_op jit(solution)/shard_map/pallas_call | solution.py:571
  22.7 0.0 collective-permute-done.5.back
  22.7 0.2 shard_map.163
  22.9 2.3 %collective-permute-start.6 = (f32[3,3,16]{2,1,0:T(4,128)S(1)}, f32[3,3,16]{2,1,0:T(4,128)S(1)}, u32[]{:S(2)}, u32[]{:S(2)}) collective-permute-start(f32[3,3,16]{2,1,0:T(4,128)S(1)} %get-tuple-element.54), channel_id=1, source_target_pairs={{2,0},{4,2},{6,4},{8,6},{10,8},{12,10},{14,12},{16,14},{18,16},{20... | collective-permute-start | bytes 1736 | tf_op jit(solution)/shard_map/ppermute | solution.py:541
  25.9 0.7 %shard_map.164 = (f32[3,256]{1,0:T(4,128)}, f32[3,256]{1,0:T(4,128)}, f32[3,256]{1,0:T(4,128)}, f32[1,256]{1,0:T(1,128)}) custom-call(s32[1]{0:T(128)S(6)} %copy.18.live_count, f32[3,256]{1,0:T(4,128)S(1)} %get-tuple-element.39.half_velocity, f32[1,256]{1,0:T(1,128)S(1)} %get-tuple-element.40.stay, f32[3,256]{1,0:T(4,128)S(1)} %get-tuple-element.30.displaced, ...), custom_call_target="tpu_custom_call" | custom-call | flops 2304 | bytes 20480 | tf_op jit(solution)/shard_map/pallas_call | solution.py:571
  26.6 2.2 %collective-permute-done.6 = f32[3,3,16]{2,1,0:T(4,128)S(1)} collective-permute-done((f32[3,3,16]{2,1,0:T(4,128)S(1)}, f32[3,3,16]{2,1,0:T(4,128)S(1)}, u32[]{:S(2)}, u32[]{:S(2)}) %collective-permute-start.6) | collective-permute-done | bytes 608 | tf_op jit(solution)/shard_map/ppermute | solution.py:541
  28.8 0.6 %copy.20 = f32[3,3,16]{2,1,0:T(4,128)} copy(f32[3,3,16]{2,1,0:T(4,128)S(1)} %collective-permute-done.6) | data formatting | bytes 1152
Async XLA Ops:
  1.4 2.5 %collective-permute-start = (f32[2,3,32]{2,1,0:T(4,128)S(1)}, f32[2,3,32]{2,1,0:T(4,128)S(1)}, u32[]{:S(2)}, u32[]{:S(2)}) collective-permute-start(f32[2,3,32]{2,1,0:T(4,128)S(1)} %get-tuple-element.31.trans_like), channel_id=1, source_target_pairs={{0,1},{1,0},{2,3},{3,2},{4,5},{5,4},{6,7},{7,6},{8,9},{9,8},{10,11... | collective-permute-start | bytes 2312 | tf_op jit(solution)/shard_map/ppermute | solution.py:557
  4.0 5.3 %collective-permute-start.1 = (f32[3,128]{1,0:T(4,128)S(1)}, f32[3,128]{1,0:T(4,128)S(1)}, u32[]{:S(2)}, u32[]{:S(2)}) collective-permute-start(f32[3,128]{1,0:T(4,128)S(1)} %get-tuple-element.33), channel_id=1, source_target_pairs={{0,2},{4,6},{8,10},{12,14},{16,18},{20,22},{24,26},{28,30},{2,0},{... | collective-permute-start | bytes 4616 | tf_op jit(solution)/shard_map/ppermute | solution.py:549
  5.9 5.8 %collective-permute-start.2 = (f32[3,128]{1,0:T(4,128)S(1)}, f32[3,128]{1,0:T(4,128)S(1)}, u32[]{:S(2)}, u32[]{:S(2)}) collective-permute-start(f32[3,128]{1,0:T(4,128)S(1)} %get-tuple-element.34), channel_id=1, source_target_pairs={{2,4},{6,8},{10,12},{14,16},{18,20},{22,24},{26,28},{4,2},{8,6},{1... | collective-permute-start | bytes 4616 | tf_op jit(solution)/shard_map/ppermute | solution.py:549
  13.8 3.2 %collective-permute-start.3 = (f32[3,128]{1,0:T(4,128)S(1)}, f32[3,128]{1,0:T(4,128)S(1)}, u32[]{:S(2)}, u32[]{:S(2)}) collective-permute-start(f32[3,128]{1,0:T(4,128)S(1)} %get-tuple-element.42), channel_id=1, source_target_pairs={{0,2},{4,6},{8,10},{12,14},{16,18},{20,22},{24,26},{28,30},{2,0},{... | collective-permute-start | bytes 4616 | tf_op jit(solution)/shard_map/ppermute | solution.py:549
  13.9 5.8 %collective-permute-start.4 = (f32[3,128]{1,0:T(4,128)S(1)}, f32[3,128]{1,0:T(4,128)S(1)}, u32[]{:S(2)}, u32[]{:S(2)}) collective-permute-start(f32[3,128]{1,0:T(4,128)S(1)} %get-tuple-element.43), channel_id=1, source_target_pairs={{2,4},{6,8},{10,12},{14,16},{18,20},{22,24},{26,28},{4,2},{8,6},{1... | collective-permute-start | bytes 4616 | tf_op jit(solution)/shard_map/ppermute | solution.py:549
  19.9 2.8 %collective-permute-start.5 = (f32[2,3,32]{2,1,0:T(4,128)S(1)}, f32[2,3,32]{2,1,0:T(4,128)S(1)}, u32[]{:S(2)}, u32[]{:S(2)}) collective-permute-start(f32[2,3,32]{2,1,0:T(4,128)S(1)} %get-tuple-element.45), channel_id=1, source_target_pairs={{0,1},{1,0},{2,3},{3,2},{4,5},{5,4},{6,7},{7,6},{8,9},{9,8},{10,11... | collective-permute-start | bytes 2312 | tf_op jit(solution)/shard_map/ppermute | solution.py:557
  22.9 5.9 %collective-permute-start.6 = (f32[3,3,16]{2,1,0:T(4,128)S(1)}, f32[3,3,16]{2,1,0:T(4,128)S(1)}, u32[]{:S(2)}, u32[]{:S(2)}) collective-permute-start(f32[3,3,16]{2,1,0:T(4,128)S(1)} %get-tuple-element.54), channel_id=1, source_target_pairs={{2,0},{4,2},{6,4},{8,6},{10,8},{12,10},{14,12},{16,14},{18,16},{20... | collective-permute-start | bytes 1736 | tf_op jit(solution)/shard_map/ppermute | solution.py:541

commit v2 on v0

--- a/solution.py
+++ b/solution.py
@@ -17,7 +17,6 @@
 pair_list = ((0, 0), (0, 1), (0, 2), (0, 3), (1, 1), (1, 2), (1, 3), (2, 2), (2, 3), (3, 3))
 degrees = 5
 lanes = 128
-highest = lax.Precision.HIGHEST
 f32 = jnp.float32
 bf16 = jnp.bfloat16
 
@@ -164,7 +163,11 @@
     shock_spots_out[1:2, :] = jnp.where(even, shock_send[0:1, :], shock_send[1:2, :])
     matrix = alpha[...]
     count = matrix.shape[0]
-    matrix_out[...] = 0.5 * (matrix + matrix.T)
+    matrix = 0.5 * (matrix + matrix.T)
+    wide = matrix_out.shape[1] // 3
+    matrix = jnp.concatenate([matrix, jnp.zeros((count, wide - count), f32)], axis=1)
+    high = matrix.astype(bf16).astype(f32)
+    matrix_out[...] = jnp.concatenate([high, high, matrix - high], axis=1).astype(bf16)
     eye = lax.broadcasted_iota(jnp.int32, (count, count), 0) == lax.broadcasted_iota(
         jnp.int32, (count, count), 1
     )
@@ -393,8 +396,10 @@
     features = jnp.concatenate(
         [packed[0, pl.ds(number, count, stride=halves), :] for number in range(halves)], axis=1
     )
+    high = features.astype(bf16).astype(f32)
+    stacked = jnp.concatenate([pad_rows(part, matrix.shape[1] // 3) for part in (high, features - high, high)], axis=0)
     slope = linear[...] + lax.dot_general(
-        matrix[...], features, (((1,), (0,)), ((), ())), precision=highest, preferred_element_type=f32
+        matrix[...], stacked.astype(bf16), (((1,), (0,)), ((), ())), preferred_element_type=f32
     )
     energy_out[...] = 0.5 * jnp.sum(features * (linear[...] + slope), axis=0, keepdims=True)
     for number in range(halves):
@@ -609,7 +614,7 @@
             shaped(2, shock_width, kind=whole),
             shaped(groups * 8, lanes, kind=whole),
             shaped(count, slots),
-            shaped(count, count),
+            shaped(count, 3 * (-(-count // 8) * 8), kind=bf16),
         ),
         (shock_send, neighbour_block, neighbour_lane, beta.reshape(1, count), alpha, trans_go),
         far=5,

time: 29.7 us -> 29.6 us (level)
  no operation moved by 1% of the time
where the time goes in v2:
time: 29.6 us; the launch traced here: 29.3 us
  starting transfers between devices  12.9 us (44%)
  waiting for transfers between devices  6.89 us (23%)
  Pallas kernels  6.31 us (21%)
  between operations  2.02 us (7%)
  local copies, waits for them, and re-layouts  0.59 us (2%)
  other arithmetic  0.58 us (2%)
    ppermute x4, starting transfers between devices, with_partner(): lax.ppermute(x, 'shock', [(i, i + 1) for i in lows] + [(i + 1, i) for i i...  8.02 us
    pallas_call x9, Pallas kernels, run_kernel(): pl.pallas_call(kernel, in_specs=[vmem] * len(args), out_specs=tuple((vmem...  6.31 us
    ppermute x4, waiting for transfers between devices, with_partner(): lax.ppermute(x, 'shock', [(i, i + 1) for i in lows] + [(i + 1, i) for i i...  3.78 us
    ppermute x1, waiting for transfers between devices, along_shock(): lax.ppermute(x, 'shock', [(i, i + by) for i in range(devices) if 0 <= i +...  2.86 us
    ppermute x2, starting transfers between devices, across(): return lax.ppermute(x, 'trans', down)  2.5 us
    ppermute x1, starting transfers between devices, along_shock(): lax.ppermute(x, 'shock', [(i, i + by) for i in range(devices) if 0 <= i +...  2.37 us
    unnamed x1, local copies, waits for them, and re-layouts  0.59 us
  transfers between devices with their start and end apart: 7, of which 4 were waited for; matrix products, arithmetic and copies ran while one was open for 2% of the time, Pallas kernels for 10%

profile of v2, /device:TPU:11, one launch (start us, length us, event | category | flops | bytes accessed | tf_op | source)
XLA Modules:
  0.0 29.3 jit_solution(6090289197799818012)
XLA Ops:
  0.6 0.8 %shard_map.155 = (f32[3,256]{1,0:T(4,128)S(1)}, f32[2,3,32]{2,1,0:T(4,128)S(1)}) custom-call(f32[3,256]{1,0:T(4,128)} %disp.1, f32[3,256]{1,0:T(4,128)} %vel.3, f32[3,256]{1,0:T(4,128)} %force.3, s32[2,32]{1,0:T(2,128)} %trans_send.3), custom_call_target="tpu_custom_call" | custom-call | tf_op jit(solution)/shard_map/pallas_call | solution.py:569
  1.4 1.2 %collective-permute-start = (f32[2,3,32]{2,1,0:T(4,128)S(1)}, f32[2,3,32]{2,1,0:T(4,128)S(1)}, u32[]{:S(2)}, u32[]{:S(2)}) collective-permute-start(f32[2,3,32]{2,1,0:T(4,128)S(1)} %get-tuple-element.31.trans_like), channel_id=1, source_target_pairs={{0,1},{1,0},{2,3},{3,2},{4,5},{5,4},{6,7},{7,6},{8,9},{9,8},{10,11... | collective-permute-start | bytes 2312 | tf_op jit(solution)/shard_map/ppermute | solution.py:555
  2.7 1.0 %shard_map.156 = (s32[2,128]{1,0:T(2,128)S(1)}, s32[56,128]{1,0:T(8,128)S(1)}, f32[50,256]{1,0:T(8,128)S(1)}, bf16[50,168]{1,0:T(8,128)(2,1)S(1)}) custom-call(s32[2,128]{1,0:T(2,128)} %shock_send.1, s32[26,256]{1,0:T(8,128)} %neighbour_block.1, s32[26,256]{1,0:T(8,128)} %neighbour_lane.1, f32[1,50]{1,0:T(1,128)} %bitcast.5, f32[50,50]{1,0:T(8,128)} %alpha.1, ...), custom_call_target="tpu_custom_call" | custom-call | flops 266240 | bytes 79872 | tf_op jit(solution)/shard_map/pallas_call | solution.py:569
  3.7 0.2 collective-permute-done.trans_in
  3.9 0.1 shard_map.157
  4.0 1.8 %collective-permute-start.1 = (f32[3,128]{1,0:T(4,128)S(1)}, f32[3,128]{1,0:T(4,128)S(1)}, u32[]{:S(2)}, u32[]{:S(2)}) collective-permute-start(f32[3,128]{1,0:T(4,128)S(1)} %get-tuple-element.33), channel_id=1, source_target_pairs={{0,2},{4,6},{8,10},{12,14},{16,18},{20,22},{24,26},{28,30},{2,0},{... | collective-permute-start | bytes 4616 | tf_op jit(solution)/shard_map/ppermute | solution.py:547
  5.9 3.1 %collective-permute-start.2 = (f32[3,128]{1,0:T(4,128)S(1)}, f32[3,128]{1,0:T(4,128)S(1)}, u32[]{:S(2)}, u32[]{:S(2)}) collective-permute-start(f32[3,128]{1,0:T(4,128)S(1)} %get-tuple-element.34), channel_id=1, source_target_pairs={{2,4},{6,8},{10,12},{14,16},{18,20},{22,24},{26,28},{4,2},{8,6},{1... | collective-permute-start | bytes 4616 | tf_op jit(solution)/shard_map/ppermute | solution.py:547
  8.9 0.4 %shard_map.158.marks = bf16[128,6656]{1,0:T(8,128)(2,1)S(1)} custom-call(s32[56,128]{1,0:T(8,128)S(1)} %get-tuple-element.35.spots), custom_call_target="tpu_custom_call" | custom-call | flops 1703936 | bytes 1703936 | tf_op jit(solution)/shard_map/pallas_call | solution.py:569
  9.3 0.0 collective-permute-done.1.from_first
  9.3 2.4 %collective-permute-done.2.from_second = f32[3,128]{1,0:T(4,128)S(1)} collective-permute-done((f32[3,128]{1,0:T(4,128)S(1)}, f32[3,128]{1,0:T(4,128)S(1)}, u32[]{:S(2)}, u32[]{:S(2)}) %collective-permute-start.2) | collective-permute-done | bytes 1568 | tf_op jit(solution)/shard_map/ppermute | solution.py:547
  11.7 2.1 %shard_map.159 = (f32[1,256]{1,0:T(1,128)S(1)}, f32[3,256]{1,0:T(4,128)S(1)}, f32[3,128]{1,0:T(4,128)S(1)}, f32[3,128]{1,0:T(4,128)S(1)}, f32[3,128]{1,0:T(4,128)S(1)}) custom-call(f32[3,256]{1,0:T(4,128)S(1)} %get-tuple-element.30.displaced, f32[2,3,32]{2,1,0:T(4,128)S(1)} %collective-permute-done.trans_in, f32[3,128]{1,0:T(4,128)S(1)} %collective-permute-done.1.from_first, ...), custom_call_target="tpu_custom_call" | custom-call | tf_op jit(solution)/shard_map/pallas_call | solution.py:569
  13.8 0.1 collective-permute-start.3
  13.9 3.1 %collective-permute-start.4 = (f32[3,128]{1,0:T(4,128)S(1)}, f32[3,128]{1,0:T(4,128)S(1)}, u32[]{:S(2)}, u32[]{:S(2)}) collective-permute-start(f32[3,128]{1,0:T(4,128)S(1)} %get-tuple-element.43), channel_id=1, source_target_pairs={{2,4},{6,8},{10,12},{14,16},{18,20},{22,24},{26,28},{4,2},{8,6},{1... | collective-permute-start | bytes 4616 | tf_op jit(solution)/shard_map/ppermute | solution.py:547
  18.2 0.0 collective-permute-done.3.back_first
  18.2 1.4 %collective-permute-done.4.back_second = f32[3,128]{1,0:T(4,128)S(1)} collective-permute-done((f32[3,128]{1,0:T(4,128)S(1)}, f32[3,128]{1,0:T(4,128)S(1)}, u32[]{:S(2)}, u32[]{:S(2)}) %collective-permute-start.4) | collective-permute-done | bytes 1568 | tf_op jit(solution)/shard_map/ppermute | solution.py:547
  19.7 0.2 shard_map.161
  19.9 1.3 %collective-permute-start.5 = (f32[2,3,32]{2,1,0:T(4,128)S(1)}, f32[2,3,32]{2,1,0:T(4,128)S(1)}, u32[]{:S(2)}, u32[]{:S(2)}) collective-permute-start(f32[2,3,32]{2,1,0:T(4,128)S(1)} %get-tuple-element.45), channel_id=1, source_target_pairs={{0,1},{1,0},{2,3},{3,2},{4,5},{5,4},{6,7},{7,6},{8,9},{9,8},{10,11... | collective-permute-start | bytes 2312 | tf_op jit(solution)/shard_map/ppermute | solution.py:555
  21.1 0.6 %add_bitcast_fusion.counts = s32[1,2]{1,0:T(1,128)} fusion(s32[1]{0:T(128)S(6)} %copy.19, s32[1]{0:T(128)S(6)} %copy.18), kind=kLoop, calls=%fused_computation | loop fusion | flops 2 | bytes 16 | tf_op jit(solution)/shard_map/reshape | solution.py:661
  21.7 0.9 %shard_map.160 = (f32[3,256]{1,0:T(4,128)S(1)}, f32[1,256]{1,0:T(1,128)S(1)}, s32[2,128]{1,0:T(2,128)S(1)}, s32[1,128]{1,0:T(1,128)S(1)}) custom-call(s32[1,2]{1,0:T(1,128)} %add_bitcast_fusion.counts, f32[3,256]{1,0:T(4,128)} %vel.3, f32[3,256]{1,0:T(4,128)} %force.3, s32[2,32]{1,0:T(2,128)} %trans_send.3, s32[1,16]{1,0:T(1,128)} %bitcast.6, ...), custom_call_target="tpu_custom_call" | custom-call | flops 10240 | bytes 102400 | tf_op jit(solution)/shard_map/pallas_call | solution.py:569
  22.6 0.0 collective-permute-done.5.back
  22.6 0.2 shard_map.162
  22.8 2.4 %collective-permute-start.6 = (f32[3,3,16]{2,1,0:T(4,128)S(1)}, f32[3,3,16]{2,1,0:T(4,128)S(1)}, u32[]{:S(2)}, u32[]{:S(2)}) collective-permute-start(f32[3,3,16]{2,1,0:T(4,128)S(1)} %get-tuple-element.54), channel_id=1, source_target_pairs={{2,0},{4,2},{6,4},{8,6},{10,8},{12,10},{14,12},{16,14},{18,16},{20... | collective-permute-start | bytes 1736 | tf_op jit(solution)/shard_map/ppermute | solution.py:539
  25.2 0.6 %shard_map.163 = (f32[3,256]{1,0:T(4,128)}, f32[3,256]{1,0:T(4,128)}, f32[3,256]{1,0:T(4,128)}, f32[1,256]{1,0:T(1,128)}) custom-call(f32[3,256]{1,0:T(4,128)S(1)} %get-tuple-element.39.half_velocity, f32[1,256]{1,0:T(1,128)S(1)} %get-tuple-element.40.kept, f32[3,256]{1,0:T(4,128)S(1)} %get-tuple-element.30.displaced, ...), custom_call_target="tpu_custom_call" | custom-call | flops 2304 | bytes 20480 | tf_op jit(solution)/shard_map/pallas_call | solution.py:569
  25.8 2.9 %collective-permute-done.6 = f32[3,3,16]{2,1,0:T(4,128)S(1)} collective-permute-done((f32[3,3,16]{2,1,0:T(4,128)S(1)}, f32[3,3,16]{2,1,0:T(4,128)S(1)}, u32[]{:S(2)}, u32[]{:S(2)}) %collective-permute-start.6) | collective-permute-done | bytes 608 | tf_op jit(solution)/shard_map/ppermute | solution.py:539
  28.7 0.6 %copy.20 = f32[3,3,16]{2,1,0:T(4,128)} copy(f32[3,3,16]{2,1,0:T(4,128)S(1)} %collective-permute-done.6) | data formatting | bytes 1152
Async XLA Ops:
  1.4 2.5 %collective-permute-start = (f32[2,3,32]{2,1,0:T(4,128)S(1)}, f32[2,3,32]{2,1,0:T(4,128)S(1)}, u32[]{:S(2)}, u32[]{:S(2)}) collective-permute-start(f32[2,3,32]{2,1,0:T(4,128)S(1)} %get-tuple-element.31.trans_like), channel_id=1, source_target_pairs={{0,1},{1,0},{2,3},{3,2},{4,5},{5,4},{6,7},{7,6},{8,9},{9,8},{10,11... | collective-permute-start | bytes 2312 | tf_op jit(solution)/shard_map/ppermute | solution.py:555
  4.0 5.3 %collective-permute-start.1 = (f32[3,128]{1,0:T(4,128)S(1)}, f32[3,128]{1,0:T(4,128)S(1)}, u32[]{:S(2)}, u32[]{:S(2)}) collective-permute-start(f32[3,128]{1,0:T(4,128)S(1)} %get-tuple-element.33), channel_id=1, source_target_pairs={{0,2},{4,6},{8,10},{12,14},{16,18},{20,22},{24,26},{28,30},{2,0},{... | collective-permute-start | bytes 4616 | tf_op jit(solution)/shard_map/ppermute | solution.py:547
  5.9 5.8 %collective-permute-start.2 = (f32[3,128]{1,0:T(4,128)S(1)}, f32[3,128]{1,0:T(4,128)S(1)}, u32[]{:S(2)}, u32[]{:S(2)}) collective-permute-start(f32[3,128]{1,0:T(4,128)S(1)} %get-tuple-element.34), channel_id=1, source_target_pairs={{2,4},{6,8},{10,12},{14,16},{18,20},{22,24},{26,28},{4,2},{8,6},{1... | collective-permute-start | bytes 4616 | tf_op jit(solution)/shard_map/ppermute | solution.py:547
  13.8 4.4 %collective-permute-start.3 = (f32[3,128]{1,0:T(4,128)S(1)}, f32[3,128]{1,0:T(4,128)S(1)}, u32[]{:S(2)}, u32[]{:S(2)}) collective-permute-start(f32[3,128]{1,0:T(4,128)S(1)} %get-tuple-element.42), channel_id=1, source_target_pairs={{0,2},{4,6},{8,10},{12,14},{16,18},{20,22},{24,26},{28,30},{2,0},{... | collective-permute-start | bytes 4616 | tf_op jit(solution)/shard_map/ppermute | solution.py:547
  13.9 5.8 %collective-permute-start.4 = (f32[3,128]{1,0:T(4,128)S(1)}, f32[3,128]{1,0:T(4,128)S(1)}, u32[]{:S(2)}, u32[]{:S(2)}) collective-permute-start(f32[3,128]{1,0:T(4,128)S(1)} %get-tuple-element.43), channel_id=1, source_target_pairs={{2,4},{6,8},{10,12},{14,16},{18,20},{22,24},{26,28},{4,2},{8,6},{1... | collective-permute-start | bytes 4616 | tf_op jit(solution)/shard_map/ppermute | solution.py:547
  19.9 2.7 %collective-permute-start.5 = (f32[2,3,32]{2,1,0:T(4,128)S(1)}, f32[2,3,32]{2,1,0:T(4,128)S(1)}, u32[]{:S(2)}, u32[]{:S(2)}) collective-permute-start(f32[2,3,32]{2,1,0:T(4,128)S(1)} %get-tuple-element.45), channel_id=1, source_target_pairs={{0,1},{1,0},{2,3},{3,2},{4,5},{5,4},{6,7},{7,6},{8,9},{9,8},{10,11... | collective-permute-start | bytes 2312 | tf_op jit(solution)/shard_map/ppermute | solution.py:555
  22.8 5.9 %collective-permute-start.6 = (f32[3,3,16]{2,1,0:T(4,128)S(1)}, f32[3,3,16]{2,1,0:T(4,128)S(1)}, u32[]{:S(2)}, u32[]{:S(2)}) collective-permute-start(f32[3,3,16]{2,1,0:T(4,128)S(1)} %get-tuple-element.54), channel_id=1, source_target_pairs={{2,0},{4,2},{6,4},{8,6},{10,8},{12,10},{14,12},{16,14},{18,16},{20... | collective-permute-start | bytes 1736 | tf_op jit(solution)/shard_map/ppermute | solution.py:539
